TPU v7x, 512 devices: a whole 4x8x8 slice. The times are simulated.
512 devices in a mesh: ctx: 64 (over z, y), head: 8 (over x, core).
Axes of the slice: x: 4, y: 8, z: 8, core: 2. Of those that a mesh axis runs over, the one named last changes fastest.
Arguments:
- queries: bfloat16 [49152, 3072], P(('ctx', 'head')), may hold values from -20 to 20
- keys: bfloat16 [49152, 3072], P(('ctx', 'head')), may hold values from -6 to 6
- values: bfloat16 [49152, 3072], P(('ctx', 'head')), may hold values from -6 to 6
- page_blocks: int32 [64, 2], replicated, may hold values from 1 to 5, as said below
- page_links: int32 [128, 16], replicated, may hold values from 0 to 127, as said below
- global_blocks: int32 [2], replicated, may hold values from 0 to 383
Outputs:
- attended: bfloat16 [49152, 3072], P(('ctx', 'head'))
Inputs may be any that keep to these rules, and one draw needn't show every extreme that they name: `page_links`: all 32 links of the pages of one ctx index name pages of distinct other ctx indices. `page_blocks`: each row sums to 6; some ctx index has a page of exactly 5 blocks.
All inputs are finite; a program needn't handle non-finite values.
Results may differ from a plain program's by a relative error of at most 0.0048.
Values may be sent and summed in bfloat16 or wider, within the bound.
A program may use at most 128 MiB of HBM per device.

v0:
```python
import jax
import jax.numpy as jnp
from jax import lax
from jax.sharding import PartitionSpec as P

HD = 128
BLK = 128
PAGES_DEV = 2
GROWS = 64
GB = 2


masked_score = -1e30


def shards(queries, keys, values, page_blocks, page_links, global_blocks):
    q_local, k_local, v_local = (
        lax.all_to_all(queries, "head", split_axis=1, concat_axis=0, tiled=True),
        lax.all_to_all(keys, "head", split_axis=1, concat_axis=0, tiled=True),
        lax.all_to_all(values, "head", split_axis=1, concat_axis=0, tiled=True),
    )
    ctx_count = lax.axis_size("ctx")
    my_index = lax.axis_index("ctx")
    rows = q_local.shape[0]
    width = q_local.shape[1]
    n_heads = width // HD
    n_blocks = rows // BLK
    link_count = page_links.shape[1]
    my_lengths = lax.dynamic_slice_in_dim(page_blocks, my_index, 1, 0)[0]
    my_starts = jnp.cumsum(my_lengths) - my_lengths
    block_ids = jnp.arange(n_blocks, dtype=jnp.int32)
    block_page = jnp.sum((block_ids[:, None] >= my_starts[None, :]).astype(jnp.int32), axis=1) - 1
    token_page = jnp.repeat(block_page, BLK)
    pair_kv = jnp.concatenate((k_local, v_local), axis=1)
    leaders = jnp.stack(
        [
            lax.dynamic_slice_in_dim(pair_kv, my_starts[page] * BLK, BLK, 0)
            for page in range(PAGES_DEV)
        ]
    )
    reader_links = page_links.reshape(ctx_count, PAGES_DEV * link_count)
    to_mine = reader_links // PAGES_DEV == my_index
    chosen = jnp.stack(
        [
            jnp.sum((to_mine & (reader_links % PAGES_DEV == page)).astype(jnp.float32), axis=1)
            for page in range(PAGES_DEV)
        ],
        axis=1,
    )
    chosen = jnp.minimum(chosen, 1.0).astype(jnp.bfloat16)
    outgoing = jnp.einsum(
        "rp,pbf->rbf", chosen, leaders, preferred_element_type=jnp.float32
    ).astype(jnp.bfloat16)
    incoming = lax.all_to_all(outgoing, "ctx", split_axis=0, concat_axis=0, tiled=True)
    my_links = lax.dynamic_slice_in_dim(page_links, my_index * PAGES_DEV, PAGES_DEV, 0)
    sources = my_links // PAGES_DEV
    span = GROWS // GB
    owners = global_blocks // n_blocks
    places = global_blocks % n_blocks
    pieces = [
        jnp.where(
            owners[i] == my_index,
            lax.dynamic_slice_in_dim(pair_kv, places[i] * BLK, span, 0).astype(jnp.float32),
            0.0,
        )
        for i in range(GB)
    ]
    global_kv = lax.psum(jnp.concatenate(pieces, 0), "ctx").astype(jnp.bfloat16)
    scale = HD ** (-0.5)
    k_own = k_local.reshape(rows, n_heads, HD)
    v_own = v_local.reshape(rows, n_heads, HD)
    g_keys = global_kv[:, :width].reshape(GROWS, n_heads, HD)
    g_values = global_kv[:, width:].reshape(GROWS, n_heads, HD)
    group_size = 1
    for count in range(1, n_blocks + 1):
        if n_blocks % count == 0 and count * BLK <= 512:
            group_size = count
    n_groups = n_blocks // group_size
    q_groups = q_local.reshape(n_groups, group_size, BLK, n_heads, HD)
    page_groups = block_page.reshape(n_groups, group_size)

    def attend_group(operands):
        q_blocks, group_page = operands
        s_own = (
            jnp.einsum("bqhd,khd->bhqk", q_blocks, k_own, preferred_element_type=jnp.float32)
            * scale
        )
        own_mask = group_page[:, None] == token_page[None, :]
        s_own = jnp.where(own_mask[:, None, None, :], s_own, masked_score)
        s_glob = (
            jnp.einsum("bqhd,ghd->bhqg", q_blocks, g_keys, preferred_element_type=jnp.float32)
            * scale
        )
        block_kv = incoming[sources[group_page]].reshape(group_size, link_count * BLK, 2 * width)
        l_keys = block_kv[:, :, :width].reshape(group_size, link_count * BLK, n_heads, HD)
        l_values = block_kv[:, :, width:].reshape(group_size, link_count * BLK, n_heads, HD)
        s_link = (
            jnp.einsum("bqhd,bkhd->bhqk", q_blocks, l_keys, preferred_element_type=jnp.float32)
            * scale
        )
        row_max = jnp.maximum(
            jnp.maximum(jnp.max(s_own, axis=3), jnp.max(s_glob, axis=3)), jnp.max(s_link, axis=3)
        )
        w_link = jnp.exp(s_link - row_max[..., None])
        total_link = jnp.sum(w_link, axis=3)
        mixed_link = jnp.einsum(
            "bhqk,bkhd->bqhd",
            w_link.astype(jnp.bfloat16),
            l_values,
            preferred_element_type=jnp.float32,
        )
        w_own = jnp.exp(s_own - row_max[..., None])
        w_glob = jnp.exp(s_glob - row_max[..., None])
        total = jnp.sum(w_own, axis=3) + jnp.sum(w_glob, axis=3) + total_link
        mixed = jnp.einsum(
            "bhqk,khd->bqhd", w_own.astype(jnp.bfloat16), v_own, preferred_element_type=jnp.float32
        )
        mixed = mixed + jnp.einsum(
            "bhqg,ghd->bqhd",
            w_glob.astype(jnp.bfloat16),
            g_values,
            preferred_element_type=jnp.float32,
        )
        mixed = mixed + mixed_link
        mixed = mixed / jnp.transpose(total, (0, 2, 1))[..., None]
        return mixed.astype(jnp.bfloat16)

    result = lax.map(attend_group, (q_groups, page_groups)).reshape(rows, width)
    return lax.all_to_all(result, "head", split_axis=0, concat_axis=1, tiled=True)


def solution(mesh):
    return jax.shard_map(
        shards,
        mesh=mesh,
        in_specs=(
            P(("ctx", "head"), None),
            P(("ctx", "head"), None),
            P(("ctx", "head"), None),
            P(),
            P(),
            P(),
        ),
        out_specs=P(("ctx", "head"), None),
        check_vma=False,
    )
```

profile of v0, /device:TPU:1, one launch (start us, length us, event | category | flops | bytes accessed | tf_op | source)
XLA Modules:
  0.0 924.7 jit_solution(17150689993805457864)
XLA Ops:
  2.0 10.3 %all-to-all-start.1 = ((bf16[96,8,384]{2,0,1:T(8,128)(2,1)}), bf16[96,8,384]{2,0,1:T(8,128)(2,1)S(1)}, u32[]{:S(2)}, u32[]{:S(2)}) async-start(bf16[96,8,384]{2,0,1:T(8,128)(2,1)} %bitcast.138), calls=%async_computation.1 | async-start | bytes 1179648 | tf_op jit(solution)/shard_map/all_to_all | solution.py:19
  14.3 8.3 all-to-all-done.1
  22.5 4.3 all-to-all-start.2
  30.4 6.6 all-to-all-done.2
  37.0 4.3 all-to-all-start
  43.5 4.6 convolution_convert_fusion
  48.1 22.8 %copy.181 = bf16[64,128,768]{2,1,0:T(8,128)(2,1)} copy(bf16[64,128,768]{2,0,1:T(8,128)(2,1)S(1)} %convolution_convert_fusion) | data formatting | bytes 25165824 | tf_op jit(solution)/shard_map/convert_element_type | solution.py:53
  71.8 12.0 %all-to-all-start.3 = ((bf16[64,128,768]{2,1,0:T(8,128)(2,1)}), bf16[64,128,768]{2,1,0:T(8,128)(2,1)}, u32[]{:S(2)}, u32[]{:S(2)}) async-start(bf16[64,128,768]{2,1,0:T(8,128)(2,1)} %copy.181), calls=%async_computation.3 | async-start | bytes 25165824 | tf_op jit(solution)/shard_map/all_to_all | solution.py:54
  89.0 634.9 %all-reduce.1 = bf16[64,768]{1,0:T(8,128)(2,1)S(1)} all-reduce(f32[64,768]{1,0:T(8,128)S(1)} %pad_maximum_fusion), channel_id=1, replica_groups=mesh['ctx'=64,'head'=8] {'ctx'}, use_global_device_ids=true, to_apply=%region_2.3 | all-reduce | flops 49152 | bytes 294912 | tf_op jit(solution)/shard_map/psum | solution.py:68
  728.6 112.3 %while.11 = (s32[]{:T(128)}, bf16[2,3,128,3,128]{4,2,1,3,0:T(8,128)(2,1)}, s32[2,3]{1,0:T(2,128)}, bf16[2,3,128,3,128]{4,2,1,3,0:T(8,128)(2,1)}, bf16[768,3,128]...) while((s32[]{:T(128)}, ...), condition=%wide.region_14.15_spmd.clone, body=%wide.region_7.14_spmd.clone.sunk | while | flops 1723615360 | bytes 118326752 | solution.py:128
  735.1 10.7 %gather_fusion.1 = bf16[48,128,768]{2,1,0:T(8,128)(2,1)} fusion(bf16[64,128,768]{2,1,0:T(8,128)(2,1)} %get-tuple-element.344, s32[1024]{0:T(1024)S(1)} %pad_clamp_fusion.5), kind=kCustom, calls=%fused_computation.1.clone.clone.1 | custom fusion | bytes 18874560 | tf_op jit(solution)/shard_map/while/body/eval_jaxpr/gather | solution.py:94
  745.7 8.4 fusion.102
  754.1 6.7 copy.247
  760.8 4.0 multiply_reduce_fusion.2
  765.1 3.9 fusion.105
  770.6 6.7 copy.249
  777.3 5.2 fusion.106
  791.1 10.9 %gather_fusion.1 = bf16[48,128,768]{2,1,0:T(8,128)(2,1)} fusion(bf16[64,128,768]{2,1,0:T(8,128)(2,1)} %get-tuple-element.344, s32[1024]{0:T(1024)S(1)} %pad_clamp_fusion.5), kind=kCustom, calls=%fused_computation.1.clone.clone.1 | custom fusion | bytes 18874560 | tf_op jit(solution)/shard_map/while/body/eval_jaxpr/gather | solution.py:94
  802.0 8.4 fusion.102
  810.4 6.7 copy.247
  817.1 4.0 multiply_reduce_fusion.2
  826.9 6.7 copy.249
  833.6 5.2 fusion.106
  843.1 80.8 %all_to_all.78 = bf16[8,96,384]{2,1,0:T(8,128)(2,1)S(1)} all-to-all(bf16[8,96,384]{2,1,0:T(8,128)(2,1)S(1)} %all_to_all.69), channel_id=1, replica_groups=mesh['ctx'=64,'head'=8] {'head'}, dimensions={0} | all-to-all | bytes 1179648 | tf_op jit(solution)/shard_map/all_to_all | solution.py:129
  (125 shorter events, 44.4 us)
Async XLA Ops:
  0.0 26.8 %copy-start = (s32[64,2]{0,1:T(2,128)S(1)}, s32[64,2]{0,1:T(2,128)}, u32[]{:S(2)}) copy-start(s32[64,2]{0,1:T(2,128)} %param.11) | copy-start | bytes 1540
  0.0 29.0 %copy-start.13 = (s32[128,16]{0,1:T(8,128)S(1)}, s32[128,16]{0,1:T(8,128)}, u32[]{:S(2)}) copy-start(s32[128,16]{0,1:T(8,128)} %param.12) | copy-start | bytes 24580
  0.0 29.5 %copy-start.9 = (bf16[96,3072]{1,0:T(8,128)(2,1)S(1)}, bf16[96,3072]{1,0:T(8,128)(2,1)}, u32[]{:S(2)}) copy-start(bf16[96,3072]{1,0:T(8,128)(2,1)} %param.8) | copy-start | bytes 1769476
  2.0 20.5 %all-to-all-start.1 = ((bf16[96,8,384]{2,0,1:T(8,128)(2,1)}), bf16[96,8,384]{2,0,1:T(8,128)(2,1)S(1)}, u32[]{:S(2)}, u32[]{:S(2)}) async-start(bf16[96,8,384]{2,0,1:T(8,128)(2,1)} %bitcast.138), calls=%async_computation.1 | async-start | bytes 1179648 | tf_op jit(solution)/shard_map/all_to_all | solution.py:19
  22.5 14.5 %all-to-all-start.2 = ((bf16[96,8,384]{2,0,1:T(8,128)(2,1)}), bf16[96,8,384]{2,0,1:T(8,128)(2,1)S(1)}, u32[]{:S(2)}, u32[]{:S(2)}) async-start(bf16[96,8,384]{2,0,1:T(8,128)(2,1)} %bitcast.137), calls=%async_computation.2 | async-start | bytes 1179648 | tf_op jit(solution)/shard_map/all_to_all | solution.py:20
  37.0 33.9 %all-to-all-start = ((bf16[96,8,384]{2,0,1:T(8,128)(2,1)}), bf16[96,8,384]{2,0,1:T(8,128)(2,1)S(1)}, u32[]{:S(2)}, u32[]{:S(2)}) async-start(bf16[96,8,384]{2,0,1:T(8,128)(2,1)} %bitcast.139), calls=%async_computation | async-start | bytes 1179648 | tf_op jit(solution)/shard_map/all_to_all | solution.py:18
  70.9 12.9 %copy-start.14 = (s32[2]{0:T(128)S(1)}, s32[2]{0:T(128)}, u32[]{:S(2)}) copy-start(s32[2]{0:T(128)} %param.13) | copy-start | bytes 28
  71.8 656.8 %all-to-all-start.3 = ((bf16[64,128,768]{2,1,0:T(8,128)(2,1)}), bf16[64,128,768]{2,1,0:T(8,128)(2,1)}, u32[]{:S(2)}, u32[]{:S(2)}) async-start(bf16[64,128,768]{2,1,0:T(8,128)(2,1)} %copy.181), calls=%async_computation.3 | async-start | bytes 25165824 | tf_op jit(solution)/shard_map/all_to_all | solution.py:54
  83.8 643.6 %copy-start.6 = (bf16[96,8,384]{2,0,1:T(8,128)(2,1)S(1)}, bf16[96,8,384]{2,0,1:T(8,128)(2,1)}, u32[]{:S(2)}) copy-start(bf16[96,8,384]{2,0,1:T(8,128)(2,1)} %copy-done.5) | copy-start | bytes 1769476
  760.8 4.0 copy-start.2
  760.8 4.0 copy-start.7
  760.8 4.3 copy-start.8
  765.1 4.9 copy-start.3
  777.3 5.2 copy-start.10
  782.5 1.0 copy-start.4
  782.6 1.0 copy-start.11
  782.6 1.0 copy-start.12
  817.1 4.0 copy-start.2
  817.1 4.0 copy-start.7
  817.1 4.3 copy-start.8
  821.3 4.9 copy-start.3
  833.6 5.2 copy-start.10
  838.8 1.0 copy-start.4
  840.9 83.8 %copy-start.1 = (s32[64,2]{0,1:T(2,128)S(1)}, s32[64,2]{0,1:T(2,128)}, u32[]{:S(2)}) copy-start(s32[64,2]{0,1:T(2,128)} %param.11) | copy-start | bytes 1540
  (3 other events, 2.9 us)
where the time goes:
time: 933 us; the launch traced here: 925 us
  blocking collectives  716 us (77%)
  local copies, waits for them, and re-layouts  112 us (12%)
  matrix products  32.5 us (3%)
  starting transfers between devices  30.9 us (3%)
  other arithmetic  15 us (2%)
  waiting for transfers between devices  14.9 us (2%)
    psum x1, blocking collectives, shards(): global_kv = lax.psum(jnp.concatenate(pieces, 0), 'ctx').astype(jnp.bfloat16)  635 us
    all_to_all x1, blocking collectives, shards(): lax.all_to_all(result, 'head', split_axis=0, concat_axis=1, tiled=True)  80.8 us
    slice x4, local copies, waits for them, and re-layouts, attend_group(): block_kv[:, :, width:].reshape(group_size, link_count * BLK, n_heads, HD)  30.1 us
    convert_element_type x1, local copies, waits for them, and re-layouts, shards(): outgoing = jnp.einsum('rp,pbf->rbf', chosen, leaders, preferred_element_t...  22.8 us
    gather x2, local copies, waits for them, and re-layouts, attend_group(): incoming[sources[group_page]]  21.6 us
  transfers between devices with their start and end apart: 4, of which 2 were waited for; matrix products, arithmetic and copies ran while one was open for 4% of the time, Pallas kernels for 0%

commit v1 on v0

v1 whole, which is shorter than its diff:
```python
import functools

import jax
import jax.numpy as jnp
from jax import lax
from jax.experimental import pallas as pl
from jax.experimental.pallas import tpu as pltpu
from jax.sharding import PartitionSpec as P

HD = 128
BLK = 128
PAGES_DEV = 2
GROWS = 64
GB = 2
RING_Y = 8
MESH = pl.DeviceIdType.MESH
MASKED = -1e30
LOG2E = 1.4426950408889634


def ring_offsets(n):
    out = []
    for d in range(1, (n + 1) // 2):
        out += [d, -d]
    if n % 2 == 0:
        out.append(n // 2)
    return out


def body(
    nz,
    ny,
    nh,
    starts_ref,
    codes_ref,
    gblk_ref,
    q_ref,
    k_ref,
    v_ref,
    out_ref,
    qx,
    kx,
    vx,
    ga,
    gb,
    picked,
    g1,
    g2,
    ks,
    vs,
    bias,
    tops,
    totals,
    mixed,
    ob,
    send_sem,
    recv_sem,
):
    rows, width = qx.shape
    rl = rows // nh
    half = BLK // 2
    span = GROWS // GB
    n_heads = width // HD
    n_blocks = rows // BLK
    me = lax.axis_index("ctx")
    mh = lax.axis_index("head")
    z, y = me // ny, me % ny
    rate = HD**-0.5 * LOG2E

    def wrap(v, n):
        return lax.rem(v + 2 * n, n)

    def ctx_at(dz, dy):
        return wrap(z + dz, nz) * ny + wrap(y + dy, ny)

    neighbours = [ctx_at(1, 0), ctx_at(-1, 0), ctx_at(0, 1), ctx_at(0, -1)]
    peers = [lax.rem(mh + r, nh) for r in range(1, nh)]
    barrier = pltpu.get_barrier_semaphore()
    for n in neighbours:
        pl.semaphore_signal(barrier, inc=1, device_id={"ctx": n}, device_id_type=MESH)
    for p in peers:
        pl.semaphore_signal(barrier, inc=1, device_id={"head": p}, device_id_type=MESH)
    pl.semaphore_wait(barrier, len(neighbours) + len(peers))

    sems = {}
    sends = []

    def sem_id(key):
        return sems.setdefault(key, len(sems))

    def remote(key, src, dst, device):
        k = sem_id(key)
        return pltpu.make_async_remote_copy(
            src_ref=src,
            dst_ref=dst,
            send_sem=send_sem.at[k],
            recv_sem=recv_sem.at[k],
            device_id=device,
            device_id_type=MESH,
        )

    def row_slot(h):
        return pl.ds(pl.multiple_of(h * rl, 16), rl)

    def col_slot(h):
        return pl.ds(pl.multiple_of(h * width, HD), width)

    def spread(name, src, dst):
        local = pltpu.make_async_copy(
            src.at[:, col_slot(mh)], dst.at[row_slot(mh), :], recv_sem.at[sem_id((name, 0))]
        )
        local.start()
        for r, p in enumerate(peers, 1):
            c = remote((name, r), src.at[:, col_slot(p)], dst.at[row_slot(mh), :], {"head": p})
            c.start()
            sends.append(c)

        def wait():
            local.wait()
            for r in range(1, nh):
                slot = dst.at[row_slot(lax.rem(mh + nh - r, nh)), :]
                remote((name, r), slot, slot, {"head": peers[r - 1]}).wait_recv()

        return wait

    wait_k = spread("k", k_ref, kx)
    wait_v = spread("v", v_ref, vx)
    wait_q = spread("q", q_ref, qx)
    wait_k()
    wait_v()

    start1 = starts_ref[me, 0]

    def choose(index, options):
        out = options[0][1]()
        for value, load in options[1:]:
            out = jnp.where(index == value, load(), out)
        return out

    for kv, src in enumerate((kx, vx)):
        for part, g in enumerate((ga, gb)):
            lo = part * half
            g[me, 0, kv] = src[lo : lo + half, :]
            g[me, 1, kv] = choose(
                start1,
                [
                    (j, lambda j=j: src[j * BLK + lo : j * BLK + lo + half, :])
                    for j in range(1, n_blocks)
                ],
            )
    owner = [gblk_ref[i] // n_blocks for i in range(GB)]
    place = [gblk_ref[i] % n_blocks for i in range(GB)]

    def load_global_candidates():
        for i in range(GB):
            for kv, src in enumerate((kx, vx)):
                g1[z, i, kv] = choose(
                    place[i],
                    [(j, lambda j=j: src[j * BLK : j * BLK + span, :]) for j in range(n_blocks)],
                )

    waited = set()
    n_picked = [0]

    class Stream:
        def __init__(s, name, ref, axis, off, kind, far=0):
            s.name, s.ref, s.axis, s.off, s.kind, s.far = name, ref, axis, off, kind, far
            s.steps = (nz if axis == "z" else ny) // 2

        def place(s, rel):
            return (rel, s.off) if s.axis == "z" else (s.off, rel)

        def slot(s, rel):
            if s.kind == "rows":
                return s.ref.at[wrap(z + rel, nz) if s.axis == "z" else wrap(y + rel, ny)]
            return s.ref.at[ctx_at(*s.place(rel))]

        def to(s, d):
            return {"ctx": ctx_at(d, 0) if s.axis == "z" else ctx_at(0, d)}

        def hops(s, d):
            return s.steps if not s.far or d == s.far else s.steps - 1

        def picks(s, d, t):
            return bool(s.far) and t == s.hops(d) - 1

        def piece(s, rel, d, t):
            ref = s.slot(rel)
            if s.far:
                return ref.at[pl.ds(0, 1)] if s.picks(d, t) else ref
            if t == s.steps - 1:
                return ref.at[pl.ds(0 if d > 0 else 1, 1)]
            return ref

        def send(s, d, t):
            if t >= s.hops(d):
                return
            if t > 0:
                s.wait(d, t - 1)
            dst = s.piece(-d * t, d, t)
            src = dst
            if s.picks(d, t):
                k = n_picked[0]
                n_picked[0] += 1
                full = s.slot(-d * t)
                code = codes_ref[s.to(d)["ctx"], ctx_at(*s.place(-d * t))]
                for kv in range(2):
                    picked[k, 0, kv] = jnp.where(code % 2 == 0, full[1, kv], full[0, kv])
                src = picked.at[k]
            c = remote((s.name, d, t), src, dst, s.to(d))
            c.start()
            sends.append(c)

        def wait(s, d, t):
            if t >= s.hops(d) or (s.name, d, t) in waited:
                return
            waited.add((s.name, d, t))
            ref = s.piece(-d * (t + 1), d, t)
            remote((s.name, d, t), ref, ref, s.to(d)).wait_recv()

        def need(s, rel):
            if abs(rel) == s.steps:
                s.wait(1, s.steps - 1)
                s.wait(-1, s.steps - 1)
            elif rel < 0:
                s.wait(1, -rel - 1)
            elif rel > 0:
                s.wait(-1, rel - 1)

        def arrivals(s, t):
            out = []
            if t >= s.steps:
                return out
            if s.far or t < s.steps - 1:
                for d in (1, -1):
                    if t < s.hops(d):
                        out.append((s, -d * (t + 1), s.picks(d, t)))
                        s.wait(d, t)
            else:
                s.wait(1, t)
                s.wait(-1, t)
                out.append((s, s.steps, False))
            return out

        def finish(s):
            for d in (1, -1):
                for t in range(s.hops(d)):
                    s.wait(d, t)

    def attend(n, first=False):
        def block(b, carry):
            at = pl.ds(pl.multiple_of(b * BLK, BLK), BLK)
            mask = jnp.where(b >= start1, bias[1:2, :n], bias[0:1, :n])
            for h in range(n_heads):
                cols = slice(h * HD, (h + 1) * HD)
                k = kx[:, cols] if first else ks[:n, cols]
                v = vx[:, cols] if first else vs[:n, cols]
                s = lax.dot_general(
                    qx[at, cols], k, (((1,), (1,)), ((), ())), preferred_element_type=jnp.float32
                )
                s = s * rate + mask
                top = jnp.max(s, axis=1, keepdims=True)
                if not first:
                    before = tops[h, at, :]
                    after = jnp.maximum(before, top)
                    top = after[:, :1]
                else:
                    after = jnp.broadcast_to(top, (BLK, HD))
                w = jnp.exp2(s - top)
                total = jnp.sum(w, axis=1, keepdims=True)
                mix = jnp.dot(w.astype(jnp.bfloat16), v, preferred_element_type=jnp.float32)
                if first:
                    totals[h, at, :] = jnp.broadcast_to(total, (BLK, HD))
                    mixed[h, at, :] = mix
                else:
                    decay = jnp.exp2(before - after)
                    totals[h, at, :] = totals[h, at, :] * decay + total
                    mixed[h, at, :] = mixed[h, at, :] * decay + mix
                tops[h, at, :] = after
            return carry

        lax.fori_loop(0, n_blocks, block, 0)

    lane = lax.broadcasted_iota(jnp.int32, (1, 2 * half), 1)

    def absorb(arrived):
        if not arrived:
            return
        level = []
        for j, (s, rel, single) in enumerate(arrived):
            ref = s.slot(rel)
            code = codes_ref[me, ctx_at(*s.place(rel))]
            at = slice(j * half, (j + 1) * half)
            for kv, dst in ((0, ks), (1, vs)):
                dst[at, :] = (
                    ref[0, kv] if single else jnp.where(code % 2 == 0, ref[1, kv], ref[0, kv])
                )
            level.append(
                [
                    jnp.where((code + 1) // 2 == page + 1, 0.0, MASKED)
                    for page in range(PAGES_DEV)
                ]
            )
        n = len(arrived) * half
        if len(arrived) % 2:
            at = slice(n, n + half)
            ks[at, :] = jnp.zeros((half, width), ks.dtype)
            vs[at, :] = jnp.zeros((half, width), vs.dtype)
            level.append([MASKED] * PAGES_DEV)
            n += half
        for page in range(PAGES_DEV):
            for j in range(0, len(level), 2):
                bias[page : page + 1, j * half : (j + 2) * half] = jnp.where(
                    lane < half, level[j][page], level[j + 1][page]
                )
        attend(n)

    def attend_own():
        token = lax.broadcasted_iota(jnp.int32, (1, rows), 1)
        for page in range(PAGES_DEV):
            bias[page : page + 1, :rows] = jnp.where(
                (token >= start1 * BLK) == (page == 1), 0.0, MASKED
            )
        attend(rows, first=True)

    def attend_global():
        for i in range(GB):
            at = slice(i * span, (i + 1) * span)
            for kv, dst in ((0, ks), (1, vs)):
                dst[at, :] = choose(
                    owner[i] % ny, [(j, lambda j=j: g2[j, i, kv]) for j in range(ny)]
                )
        for page in range(PAGES_DEV):
            bias[page : page + 1, :GROWS] = jnp.zeros((1, GROWS), jnp.float32)
        attend(GROWS)

    a1 = Stream("a1", ga, "z", 0, "pages")
    b1 = Stream("b1", gb, "y", 0, "pages")
    za, yb = ring_offsets(nz), ring_offsets(ny)
    a2 = {o: Stream(("a2", o), ga, "y", o, "pages", 1 - 2 * (i % 2)) for i, o in enumerate([0] + za)}
    b2 = {o: Stream(("b2", o), gb, "z", o, "pages", 1 - 2 * (i % 2)) for i, o in enumerate([0] + yb)}
    r1 = Stream("r1", g1, "z", 0, "rows")
    r2 = Stream("r2", g2, "y", 0, "rows")

    def pairs(offs):
        out = []
        while len(offs) > 3:
            out.append(offs[:2])
            offs = offs[2:]
        return out + ([offs] if offs else [])

    za, yb = pairs(za), pairs(yb)
    groups = [[a1, b1, a2[0], b2[0]]]
    for i in range(max(len(za), len(yb))):
        g = [a2[o] for o in (za[i] if i < len(za) else [])]
        groups.append(g + [b2[o] for o in (yb[i] if i < len(yb) else [])])
    groups[min(1, len(groups) - 2)].append(r1)
    groups[-1].append(r2)
    pending = []
    for gi, g in enumerate(groups):
        for t in range(max(s.steps for s in g)):
            if r1 in g and t == 0:
                load_global_candidates()
            if gi == len(groups) - 1 and t == 0:
                r1.finish()
                for i in range(GB):
                    for kv in range(2):
                        g2[y, i, kv] = choose(
                            owner[i] // ny, [(j, lambda j=j: g1[j, i, kv]) for j in range(nz)]
                        )
            for s in g:
                if t == 0 and s.off != 0:
                    (a1 if s.axis == "y" else b1).need(s.off)
                for d in (1, -1):
                    s.send(d, t)
            if gi == 0 and t == 0:
                wait_q()
                attend_own()
            arrived = []
            for s, ts in pending:
                arrived += s.arrivals(ts)
            absorb(arrived)
            pending = [(s, t) for s in g if s.kind == "pages"]
    r2.finish()
    attend_global()
    arrived = []
    for s, ts in pending:
        arrived += s.arrivals(ts)
    absorb(arrived)
    for s in [a1, b1, r1] + list(a2.values()) + list(b2.values()):
        s.finish()

    for h in range(n_heads):
        cols = slice(h * HD, (h + 1) * HD)
        ob[:, cols] = (mixed[h] / totals[h]).astype(jnp.bfloat16)

    local = pltpu.make_async_copy(
        ob.at[row_slot(mh), :], out_ref.at[:, col_slot(mh)], recv_sem.at[sem_id(("o", 0))]
    )
    local.start()
    for r, p in enumerate(peers, 1):
        c = remote(("o", r), ob.at[row_slot(p), :], out_ref.at[:, col_slot(mh)], {"head": p})
        c.start()
        sends.append(c)
    local.wait()
    for r in range(1, nh):
        slot = out_ref.at[:, col_slot(lax.rem(mh + nh - r, nh))]
        remote(("o", r), slot, slot, {"head": peers[r - 1]}).wait_recv()
    for c in sends:
        c.wait_send()


def shards(nz, ny, nh, queries, keys, values, page_blocks, page_links, global_blocks):
    rl, full = queries.shape
    rows, width = rl * nh, full // nh
    n_ctx = nz * ny
    n_heads = width // HD
    half = BLK // 2
    span = GROWS // GB
    bf, f32 = jnp.bfloat16, jnp.float32
    reader = jnp.arange(PAGES_DEV, dtype=jnp.int32)[None, :, None]
    links = page_links.reshape(n_ctx, PAGES_DEV, -1)
    value = 1 + links % PAGES_DEV + PAGES_DEV * reader
    source = jnp.arange(n_ctx, dtype=jnp.int32)
    codes = jnp.sum(
        jnp.where((links // PAGES_DEV)[..., None] == source, value[..., None], 0), axis=(1, 2)
    )
    n_sems = 4 * nh + (nz + ny) + nz * ny * 2 + (nz + ny)
    most = max(rows, 12 * half)
    smem = pl.BlockSpec(memory_space=pltpu.SMEM)
    hbm = pl.BlockSpec(memory_space=pl.ANY)
    return pl.pallas_call(
        functools.partial(body, nz, ny, nh),
        out_shape=jax.ShapeDtypeStruct((rl, full), bf),
        in_specs=[smem, smem, smem, hbm, hbm, hbm],
        out_specs=hbm,
        scratch_shapes=[
            pltpu.VMEM((rows, width), bf),
            pltpu.VMEM((rows, width), bf),
            pltpu.VMEM((rows, width), bf),
            pltpu.VMEM((n_ctx, PAGES_DEV, 2, half, width), bf),
            pltpu.VMEM((n_ctx, PAGES_DEV, 2, half, width), bf),
            pltpu.VMEM((2 * (nz + ny), 1, 2, half, width), bf),
            pltpu.VMEM((nz, GB, 2, span, width), bf),
            pltpu.VMEM((ny, GB, 2, span, width), bf),
            pltpu.VMEM((most, width), bf),
            pltpu.VMEM((most, width), bf),
            pltpu.VMEM((PAGES_DEV, most), f32),
            pltpu.VMEM((n_heads, rows, HD), f32),
            pltpu.VMEM((n_heads, rows, HD), f32),
            pltpu.VMEM((n_heads, rows, HD), f32),
            pltpu.VMEM((rows, width), bf),
            pltpu.SemaphoreType.DMA((n_sems,)),
            pltpu.SemaphoreType.DMA((n_sems,)),
        ],
        compiler_params=pltpu.CompilerParams(
            collective_id=0, has_side_effects=True, vmem_limit_bytes=60 * 1024 * 1024
        ),
        name="page_attention",
    )(page_blocks, codes, global_blocks, queries, keys, values)


def solution(mesh):
    nh = mesh.shape["head"]
    ny = RING_Y
    nz = mesh.shape["ctx"] // ny
    return jax.shard_map(
        functools.partial(shards, nz, ny, nh),
        mesh=mesh,
        in_specs=(
            P(("ctx", "head"), None),
            P(("ctx", "head"), None),
            P(("ctx", "head"), None),
            P(),
            P(),
            P(),
        ),
        out_specs=P(("ctx", "head"), None),
        check_vma=False,
    )
```

time: 933 us -> 223 us (0.24)
  blocking collectives: 716 us -> 0 us
  Pallas kernels: 0 us -> 218 us
  local copies, waits for them, and re-layouts: 112 us -> 3.4 us
  matrix products: 32.5 us -> 0 us
  starting transfers between devices: 30.9 us -> 0 us
  waiting for transfers between devices: 14.9 us -> 0 us
  other arithmetic: 15 us -> 1.57 us
    psum x1 -> x0, blocking collectives: 635 us -> none  [shards(): global_kv = lax.psum(jnp.concatenate(pieces, 0), 'ctx').astype(jnp.bfloat16)]
    pallas_call x0 -> x1, Pallas kernels: none -> 218 us  [shards(): pl.pallas_call(functools.partial(body, nz, ny, nh), out_shape=jax.ShapeDt...]
    all_to_all x1 -> x0, blocking collectives: 80.8 us -> none  [shards(): lax.all_to_all(result, 'head', split_axis=0, concat_axis=1, tiled=True)]
    slice x8 -> x0, local copies, waits for them, and re-layouts: 44.7 us -> none  [the longest x4 30.1 us: attend_group(): block_kv[:, :, width:].reshape(group_size, link_count * BLK, n_heads, HD)]
    dot_general x13 -> x0, matrix products: 32.5 us -> none  [the longest x2 10.4 us: attend_group(): jnp.einsum('bhqk,bkhd->bqhd', w_link.astype(jnp.bfloat16), l_values, pref...]
    all_to_all x4 -> x0, starting transfers between devices: 30.9 us -> none  [the longest x1 12 us: shards(): lax.all_to_all(outgoing, 'ctx', split_axis=0, concat_axis=0, tiled=True)]
    convert_element_type x1 -> x0, local copies, waits for them, and re-layouts: 22.8 us -> none  [shards(): outgoing = jnp.einsum('rp,pbf->rbf', chosen, leaders, preferred_element_t...]
    gather x4 -> x0, local copies, waits for them, and re-layouts: 22.7 us -> none  [the longest x2 21.6 us: attend_group(): incoming[sources[group_page]]]
  transfers between devices with their start and end apart: 4 -> 0, of which waited for: 2 -> 0; matrix products, arithmetic and copies ran while one was open for 4% -> 0% of each run, Pallas kernels for 0% -> 0%
where the time goes in v1:
time: 223 us
  Pallas kernels  218 us (98%)
  local copies, waits for them, and re-layouts  3.4 us (2%)
    pallas_call x1, Pallas kernels, shards(): pl.pallas_call(functools.partial(body, nz, ny, nh), out_shape=jax.ShapeDt...  218 us

profile of v1, /device:TPU:1, one launch (start us, length us, event | category | flops | bytes accessed | tf_op | source)
XLA Modules:
  0.0 222.7 jit_solution(58820658221549145)
XLA Ops:
  0.0 0.0 copy-start.1
  0.0 0.7 copy-done.1
  0.7 0.0 copy-start
  0.7 0.7 copy.13.starts_ref
  1.4 0.0 copy-done
  1.4 0.1 copy.12
  1.5 0.2 and_select_fusion.1
  1.7 1.3 select_reduce_fusion.codes_ref
  3.1 217.8 %page_attention.1 = bf16[96,3072]{1,0:T(8,128)(2,1)} custom-call(s32[64,2]{1,0:T(8,128)} %copy.13.starts_ref, s32[64,64]{1,0:T(8,128)} %select_reduce_fusion.codes_ref, s32[2]{0:T(128)} %gblk_ref.1, bf16[96,3072]{1,0:T(8,128)(2,1)} %q_ref.1, bf16[96,3072]{1,0:T(8,128)(2,1)} %k_ref.1, bf16[96,3072]{1,0:T(8,128)(2,1)} %v_ref.1), custom_call_target="tpu_custom_call" | custom-call | tf_op jit(solution)/shard_map/page_attention/pallas_call | solution.py:432
  220.8 1.9 copy.15
  (1 shorter events, 0.0 us)
Async XLA Ops:
  0.0 0.7 copy-start.1
  0.7 0.7 copy-start

commit v2 on v1

v2 whole, which is shorter than its diff:
```python
import functools

import jax
import jax.numpy as jnp
from jax import lax
from jax.experimental import pallas as pl
from jax.experimental.pallas import tpu as pltpu
from jax.sharding import PartitionSpec as P

HD = 128
BLK = 128
PAGES_DEV = 2
GROWS = 64
GB = 2
RING_Y = 8
MESH = pl.DeviceIdType.MESH
MASKED = -1e30
LOG2E = 1.4426950408889634


def ring_offsets(n):
    out = []
    for d in range(1, (n + 1) // 2):
        out += [d, -d]
    if n % 2 == 0:
        out.append(n // 2)
    return out


def body(
    nz,
    ny,
    nh,
    codes_ref,
    gblk_ref,
    q_ref,
    k_ref,
    v_ref,
    out_ref,
    qx,
    kx,
    vx,
    ga,
    gb,
    picked,
    own_piece,
    got_z,
    got_y,
    picked_rows,
    ks,
    vt,
    marks,
    qmarks,
    tops,
    totals,
    mixed,
    ob,
    send_sem,
    recv_sem,
):
    rows, width = qx.shape
    rl = rows // nh
    half = BLK // 2
    span = GROWS // GB
    n_heads = width // HD
    n_blocks = rows // BLK
    me = lax.axis_index("ctx")
    mh = lax.axis_index("head")
    z, y = me // ny, me % ny
    rate = HD**-0.5 * LOG2E

    def wrap(v, n):
        return lax.rem(v + 2 * n, n)

    def ctx_at(dz, dy):
        return wrap(z + dz, nz) * ny + wrap(y + dy, ny)

    neighbours = [ctx_at(0, 1), ctx_at(0, -1)] + [ctx_at(r, 0) for r in range(1, nz)]
    peers = [lax.rem(mh + r, nh) for r in range(1, nh)]
    barrier = pltpu.get_barrier_semaphore()
    for n in neighbours:
        pl.semaphore_signal(barrier, inc=1, device_id={"ctx": n}, device_id_type=MESH)
    for p in peers:
        pl.semaphore_signal(barrier, inc=1, device_id={"head": p}, device_id_type=MESH)
    pl.semaphore_wait(barrier, len(neighbours) + len(peers))

    sems = {}
    sends = []

    def sem_id(key):
        return sems.setdefault(key, len(sems))

    def remote(key, src, dst, device):
        k = sem_id(key)
        return pltpu.make_async_remote_copy(
            src_ref=src,
            dst_ref=dst,
            send_sem=send_sem.at[k],
            recv_sem=recv_sem.at[k],
            device_id=device,
            device_id_type=MESH,
        )

    def row_slot(h):
        return pl.ds(pl.multiple_of(h * rl, 16), rl)

    def col_slot(h):
        return pl.ds(pl.multiple_of(h * width, HD), width)

    def spread(name, src, dst):
        local = pltpu.make_async_copy(
            src.at[:, col_slot(mh)], dst.at[row_slot(mh), :], recv_sem.at[sem_id((name, 0))]
        )
        local.start()
        for r, p in enumerate(peers, 1):
            c = remote((name, r), src.at[:, col_slot(p)], dst.at[row_slot(mh), :], {"head": p})
            c.start()
            sends.append(c)

        def wait():
            local.wait()
            for r in range(1, nh):
                slot = dst.at[row_slot(lax.rem(mh + nh - r, nh)), :]
                remote((name, r), slot, slot, {"head": peers[r - 1]}).wait_recv()

        return wait

    wait_k = spread("k", k_ref, kx)
    wait_v = spread("v", v_ref, vx)
    wait_q = spread("q", q_ref, qx)
    wait_k()
    wait_v()

    start1 = codes_ref[me, me]

    def choose(index, options):
        out = options[0][1]()
        for value, load in options[1:]:
            out = jnp.where(index == value, load(), out)
        return out

    for kv, src in enumerate((kx, vx)):
        for part, g in enumerate((ga, gb)):
            lo = part * half
            g[me, 0, kv] = src[lo : lo + half, :]
            g[me, 1, kv] = choose(
                start1,
                [
                    (j, lambda j=j: src[j * BLK + lo : j * BLK + lo + half, :])
                    for j in range(1, n_blocks)
                ],
            )
    owner = [gblk_ref[i] // n_blocks for i in range(GB)]
    place = [gblk_ref[i] % n_blocks for i in range(GB)]

    piece_rows = own_piece.shape[1]
    per = span // piece_rows
    pieces = [(i, kv, r) for i in range(GB) for kv in range(2) for r in range(per)]

    def send_candidates():
        for n, (i, kv, r) in enumerate(pieces):
            src = (kx, vx)[kv]
            lo = r * piece_rows
            own_piece[n] = choose(
                place[i],
                [
                    (j, lambda j=j: src[j * BLK + lo : j * BLK + lo + piece_rows, :])
                    for j in range(n_blocks)
                ],
            )
        got_z[z] = own_piece[z]
        for r in range(1, nz):
            zz = wrap(z + r, nz)
            c = remote(("g", r), own_piece.at[zz], got_z.at[z], {"ctx": zz * ny + y})
            c.start()
            sends.append(c)

    def pick_z():
        for r in range(1, nz):
            ref = got_z.at[wrap(z - r, nz)]
            remote(("g", r), ref, ref, {"ctx": ctx_at(-r, 0)}).wait_recv()
        o = owner[0]
        for i in range(1, GB):
            o = jnp.where(z >= i * (nz // GB), owner[i], o)
        got_y[y] = choose(o // ny, [(j, lambda j=j: got_z[j]) for j in range(nz)])

    def pick_y():
        r1.finish()
        o = owner[0]
        for i in range(1, GB):
            o = jnp.where(z >= i * (nz // GB), owner[i], o)
        picked_rows[z] = choose(o % ny, [(j, lambda j=j: got_y[j]) for j in range(ny)])

    def global_entries():
        r2.finish()

        def load(lo):
            out = []
            for kv in range(2):
                own = [n for n, q in enumerate(pieces) if q[1] == kv]
                out.append(jnp.concatenate([picked_rows[n] for n in own], axis=0)[lo : lo + half])
            return out

        return [
            (functools.partial(load, lo), [0.0] * PAGES_DEV) for lo in range(0, GROWS, half)
        ]

    waited = set()
    n_picked = [0]

    class Stream:
        def __init__(s, name, ref, axis, off, kind, far=0):
            s.name, s.ref, s.axis, s.off, s.kind, s.far = name, ref, axis, off, kind, far
            s.steps = (nz if axis == "z" else ny) // 2
            s.single = kind == "pages" and far != 0

        def place(s, rel):
            return (rel, s.off) if s.axis == "z" else (s.off, rel)

        def slot(s, rel):
            if s.kind == "rows":
                return s.ref.at[wrap(z + rel, nz) if s.axis == "z" else wrap(y + rel, ny)]
            return s.ref.at[ctx_at(*s.place(rel))]

        def to(s, d):
            return {"ctx": ctx_at(d, 0) if s.axis == "z" else ctx_at(0, d)}

        def hops(s, d):
            return s.steps if not s.far or d == s.far else s.steps - 1

        def picks(s, d, t):
            return s.single and t == s.hops(d) - 1

        def piece(s, rel, d, t):
            ref = s.slot(rel)
            if s.far:
                return ref.at[pl.ds(0, 1)] if s.picks(d, t) else ref
            if t == s.steps - 1:
                return ref.at[pl.ds(0 if d > 0 else 1, 1)]
            return ref

        def send(s, d, t):
            if t >= s.hops(d):
                return
            if t > 0:
                s.wait(d, t - 1)
            dst = s.piece(-d * t, d, t)
            src = dst
            if s.picks(d, t):
                k = n_picked[0]
                n_picked[0] += 1
                full = s.slot(-d * t)
                code = codes_ref[s.to(d)["ctx"], ctx_at(*s.place(-d * t))]
                for kv in range(2):
                    picked[k, 0, kv] = jnp.where(code % 2 == 0, full[1, kv], full[0, kv])
                src = picked.at[k]
            c = remote((s.name, d, t), src, dst, s.to(d))
            c.start()
            sends.append(c)

        def wait(s, d, t):
            if t >= s.hops(d) or (s.name, d, t) in waited:
                return
            waited.add((s.name, d, t))
            ref = s.piece(-d * (t + 1), d, t)
            remote((s.name, d, t), ref, ref, s.to(d)).wait_recv()

        def need(s, rel):
            if abs(rel) == s.steps:
                s.wait(1, s.steps - 1)
                s.wait(-1, s.steps - 1)
            elif rel < 0:
                s.wait(1, -rel - 1)
            elif rel > 0:
                s.wait(-1, rel - 1)

        def arrivals(s, t):
            out = []
            if t >= s.steps:
                return out
            if s.far or t < s.steps - 1:
                for d in (1, -1):
                    if t < s.hops(d):
                        out.append(page_entry(s, -d * (t + 1), s.picks(d, t)))
                        s.wait(d, t)
            else:
                s.wait(1, t)
                s.wait(-1, t)
                out.append(page_entry(s, s.steps, False))
            return out

        def finish(s):
            for d in (1, -1):
                for t in range(s.hops(d)):
                    s.wait(d, t)

    out_sems = [sem_id(("o", r)) for r in range(nh)]
    local = pltpu.make_async_copy(
        ob.at[row_slot(mh), :], out_ref.at[:, col_slot(mh)], recv_sem.at[out_sems[0]]
    )

    def hand_out(b):
        for h in range(n_heads):
            for lo in range(b * tile, (b + 1) * tile, BLK):
                at = slice(lo, lo + BLK)
                out = mixed[h, :, at] / totals[h, :, at]
                ob[at, h * HD : (h + 1) * HD] = out.T.astype(jnp.bfloat16)
        for p in range(b * tile // rl, (b + 1) * tile // rl):

            @pl.when(mh == p)
            def _():
                local.start()

            @pl.when(mh != p)
            def _():
                at = out_sems[0] + lax.rem(p - mh + nh, nh)
                pltpu.make_async_remote_copy(
                    src_ref=ob.at[row_slot(p), :],
                    dst_ref=out_ref.at[:, col_slot(mh)],
                    send_sem=send_sem.at[at],
                    recv_sem=recv_sem.at[at],
                    device_id={"head": jnp.int32(p)},
                    device_id_type=MESH,
                ).start()

    tile = 2 * BLK if rows % (2 * BLK) == 0 else rows

    def page_marks(n, first_row):
        row = lax.broadcasted_iota(jnp.int32, (n, HD), 0) + first_row
        page = jnp.where(row >= start1 * BLK, 1, 0)
        return page == lax.broadcasted_iota(jnp.int32, (n, HD), 1)

    def attend(n, keys, first=False, last=False):
        def block(b, carry):
            at = pl.ds(pl.multiple_of(b * tile, tile), tile)
            for h in range(n_heads):
                cols = slice(h * HD, (h + 1) * HD)
                s = lax.dot_general(
                    jnp.concatenate((keys[:n, cols], marks[:n, :]), axis=1),
                    jnp.concatenate((qx[at, cols], qmarks[at, :]), axis=1),
                    (((1,), (1,)), ((), ())),
                    preferred_element_type=jnp.float32,
                )
                s = s * rate
                top = jnp.max(s, axis=0, keepdims=True)
                if not first:
                    before = tops[h, :, at]
                    top = jnp.maximum(before, top)
                w = jnp.exp2(s - top)
                total = jnp.sum(w, axis=0, keepdims=True)
                mix = jnp.dot(
                    vt[cols, :n], w.astype(jnp.bfloat16), preferred_element_type=jnp.float32
                )
                if not first:
                    decay = jnp.exp2(before - top)
                    total = totals[h, :, at] * decay + total
                    mix = mixed[h, :, at] * decay + mix
                totals[h, :, at] = total
                mixed[h, :, at] = mix
                tops[h, :, at] = top
            return carry

        if not last:
            lax.fori_loop(0, rows // tile, block, 0)
            return
        for b in range(rows // tile):
            block(b, 0)
            hand_out(b)

    lane = lax.broadcasted_iota(jnp.int32, (half, HD), 1)

    def absorb(entries, last=False):
        if not entries:
            return
        zero = jnp.zeros((half, width), jnp.bfloat16)
        if len(entries) % 2:
            entries = entries + [(lambda: (zero, zero), [MASKED] * PAGES_DEV)]
        for j in range(0, len(entries), 2):
            pair = []
            for i, (load, level) in enumerate(entries[j : j + 2], j):
                k, v = load()
                ks[i * half : (i + 1) * half, :] = k
                marks[i * half : (i + 1) * half, :] = jnp.where(
                    lane == 0, level[0], jnp.where(lane == 1, level[1], 0.0)
                ).astype(jnp.bfloat16)
                pair.append(v)
            vt[:, j * half : (j + 2) * half] = jnp.concatenate(pair, axis=0).T
        attend(len(entries) * half, ks, last=last)

    def page_entry(s, rel, single):
        ref = s.slot(rel)
        code = codes_ref[me, ctx_at(*s.place(rel))]

        def load():
            if single:
                return ref[0, 0], ref[0, 1]
            return [jnp.where(code % 2 == 0, ref[1, kv], ref[0, kv]) for kv in range(2)]

        level = [
            jnp.where((code + 1) // 2 == page + 1, 0.0, MASKED) for page in range(PAGES_DEV)
        ]
        return load, level

    def attend_own():
        qmarks[...] = jnp.where(page_marks(rows, 0), 1.0, 0.0).astype(jnp.bfloat16)
        marks[:rows, :] = jnp.where(
            page_marks(rows, 0) | (lax.broadcasted_iota(jnp.int32, (rows, HD), 1) >= PAGES_DEV),
            0.0,
            MASKED,
        ).astype(jnp.bfloat16)
        for b in range(n_blocks):
            at = slice(b * BLK, (b + 1) * BLK)
            vt[:, at] = vx[at, :].T
        attend(rows, kx, first=True)

    a1 = Stream("a1", ga, "z", 0, "pages")
    b1 = Stream("b1", gb, "y", 0, "pages")
    za, yb = ring_offsets(nz), ring_offsets(ny)
    a2 = {o: Stream(("a2", o), ga, "y", o, "pages", 1 - 2 * (i % 2)) for i, o in enumerate([0] + za)}
    b2 = {o: Stream(("b2", o), gb, "z", o, "pages", 1 - 2 * (i % 2)) for i, o in enumerate([0] + yb)}
    r1 = Stream("r1", got_y, "y", 0, "rows", 1)
    r2 = Stream("r2", picked_rows, "z", 0, "rows", -1)

    def pairs(offs):
        out = []
        while len(offs) > 3:
            out.append(offs[:2])
            offs = offs[2:]
        return out + ([offs] if offs else [])

    za, yb = pairs(za), pairs(yb)
    groups = [[a1, b1, a2[0], b2[0]]]
    for i in range(max(len(za), len(yb))):
        g = [a2[o] for o in (za[i] if i < len(za) else [])]
        groups.append(g + [b2[o] for o in (yb[i] if i < len(yb) else [])])
    rounds = []
    for gi, g in enumerate(groups):
        for t in range(max(s.steps for s in g)):
            if gi > 0 and t == 0 and len(rounds) > 1:
                rounds[-1] += [(s, t) for s in g]
            else:
                rounds.append([(s, t) for s in g])
    last = len(rounds) - 1
    z_round, y_round = min(2, last), min(6, last)
    row_streams = []

    def push_rows(everything=False):
        for entry in row_streams:
            while entry[1] < entry[0].steps:
                for d in (1, -1):
                    entry[0].send(d, entry[1])
                entry[1] += 1
                if not everything:
                    break

    pending = []
    globals_done = False
    for n, todo in enumerate(rounds):
        for s, t in todo:
            if t == 0 and s.off != 0:
                (a1 if s.axis == "y" else b1).need(s.off)
            for d in (1, -1):
                s.send(d, t)
        if n == 0:
            send_candidates()
        if n == z_round:
            pick_z()
            row_streams.append([r1, 0])
        if n == y_round:
            push_rows(True)
            pick_y()
            row_streams.append([r2, 0])
        push_rows()
        if n == min(1, last):
            wait_q()
            attend_own()
        if n > 0:
            arrived = []
            for s, t in pending:
                arrived += s.arrivals(t)
            if n == y_round + 5:
                push_rows(True)
                arrived += global_entries()
                globals_done = True
            absorb(arrived)
        pending = todo
    arrived = []
    for s, t in pending:
        arrived += s.arrivals(t)
    if not globals_done:
        push_rows(True)
        arrived += global_entries()
    absorb(arrived, True)
    for s in [a1, b1, r1] + list(a2.values()) + list(b2.values()):
        s.finish()

    local.wait()
    for r in range(1, nh):
        slot = out_ref.at[:, col_slot(lax.rem(mh + nh - r, nh))]
        remote(("o", r), slot, slot, {"head": peers[r - 1]}).wait_recv()
        mine = ob.at[row_slot(peers[r - 1]), :]
        remote(("o", r), mine, mine, {"head": peers[r - 1]}).wait_send()
    for c in sends:
        c.wait_send()


def shards(nz, ny, nh, queries, keys, values, page_blocks, page_links, global_blocks):
    rl, full = queries.shape
    rows, width = rl * nh, full // nh
    n_ctx = nz * ny
    n_heads = width // HD
    half = BLK // 2
    span = GROWS // GB
    bf, f32 = jnp.bfloat16, jnp.float32
    reader = jnp.arange(PAGES_DEV, dtype=jnp.int32)[None, :, None]
    links = page_links.reshape(n_ctx, PAGES_DEV, -1)
    value = 1 + links % PAGES_DEV + PAGES_DEV * reader
    source = jnp.arange(n_ctx, dtype=jnp.int32)
    codes = jnp.sum(
        jnp.where((links // PAGES_DEV)[..., None] == source, value[..., None], 0), axis=(1, 2)
    )
    codes = jnp.where(source[:, None] == source, page_blocks[:, :1], codes)
    n_sems = 4 * nh + 3 * (nz + ny) + nz * ny * 2
    piece_rows = span * GB * 2 // nz
    most = max(rows, 16 * half)
    smem = pl.BlockSpec(memory_space=pltpu.SMEM)
    hbm = pl.BlockSpec(memory_space=pl.ANY)
    return pl.pallas_call(
        functools.partial(body, nz, ny, nh),
        out_shape=jax.ShapeDtypeStruct((rl, full), bf),
        in_specs=[smem, smem, hbm, hbm, hbm],
        out_specs=hbm,
        scratch_shapes=[
            pltpu.VMEM((rows, width), bf),
            pltpu.VMEM((rows, width), bf),
            pltpu.VMEM((rows, width), bf),
            pltpu.VMEM((n_ctx, PAGES_DEV, 2, half, width), bf),
            pltpu.VMEM((n_ctx, PAGES_DEV, 2, half, width), bf),
            pltpu.VMEM((2 * (nz + ny), 1, 2, half, width), bf),
            pltpu.VMEM((nz, piece_rows, width), bf),
            pltpu.VMEM((nz, piece_rows, width), bf),
            pltpu.VMEM((ny, piece_rows, width), bf),
            pltpu.VMEM((nz, piece_rows, width), bf),
            pltpu.VMEM((most, width), bf),
            pltpu.VMEM((width, most), bf),
            pltpu.VMEM((most, HD), bf),
            pltpu.VMEM((rows, HD), bf),
            pltpu.VMEM((n_heads, 1, rows), f32),
            pltpu.VMEM((n_heads, 1, rows), f32),
            pltpu.VMEM((n_heads, HD, rows), f32),
            pltpu.VMEM((rows, width), bf),
            pltpu.SemaphoreType.DMA((n_sems,)),
            pltpu.SemaphoreType.DMA((n_sems,)),
        ],
        compiler_params=pltpu.CompilerParams(
            collective_id=0, has_side_effects=True, vmem_limit_bytes=60 * 1024 * 1024
        ),
        name="page_attention",
    )(codes, global_blocks, queries, keys, values)


def solution(mesh):
    nh = mesh.shape["head"]
    ny = RING_Y
    nz = mesh.shape["ctx"] // ny
    return jax.shard_map(
        functools.partial(shards, nz, ny, nh),
        mesh=mesh,
        in_specs=(
            P(("ctx", "head"), None),
            P(("ctx", "head"), None),
            P(("ctx", "head"), None),
            P(),
            P(),
            P(),
        ),
        out_specs=P(("ctx", "head"), None),
        check_vma=False,
    )
```

time: 223 us -> 180 us (0.81)
  Pallas kernels: 218 us -> 174 us
    pallas_call x1, Pallas kernels: 218 us -> 174 us  [shards(): pl.pallas_call(functools.partial(body, nz, ny, nh), out_shape=jax.ShapeDt...]
where the time goes in v2:
time: 180 us; the launch traced here: 179 us
  Pallas kernels  174 us (97%)
  local copies, waits for them, and re-layouts  3.39 us (2%)
    pallas_call x1, Pallas kernels, shards(): pl.pallas_call(functools.partial(body, nz, ny, nh), out_shape=jax.ShapeDt...  174 us

profile of v2, /device:TPU:1, one launch (start us, length us, event | category | flops | bytes accessed | tf_op | source)
XLA Modules:
  0.0 178.9 jit_solution(14835993663777639104)
XLA Ops:
  0.0 0.7 slice_bitcast_fusion
  0.7 0.8 copy.10
  1.5 0.2 and_select_fusion.1
  1.7 0.7 select_reduce_fusion
  2.4 0.7 fusion.2.codes_ref
  3.1 173.9 %page_attention.1 = bf16[96,3072]{1,0:T(8,128)(2,1)} custom-call(s32[64,64]{1,0:T(8,128)} %fusion.2.codes_ref, s32[2]{0:T(128)} %gblk_ref.1, bf16[96,3072]{1,0:T(8,128)(2,1)} %q_ref.1, bf16[96,3072]{1,0:T(8,128)(2,1)} %k_ref.1, bf16[96,3072]{1,0:T(8,128)(2,1)} %v_ref.1), custom_call_target="tpu_custom_call" | custom-call | tf_op jit(solution)/shard_map/page_attention/pallas_call | solution.py:528
  177.0 1.9 %copy.12 = bf16[96,3072]{1,0:T(8,128)(2,1)} copy(bf16[96,3072]{1,0:T(8,128)(2,1)} %page_attention.1) | data formatting | bytes 1179648
  (1 shorter events, 0.0 us)

commit v3 on v2

--- a/solution.py
+++ b/solution.py
@@ -429,17 +429,26 @@
         return out + ([offs] if offs else [])
 
     za, yb = pairs(za), pairs(yb)
-    groups = [[a1, b1, a2[0], b2[0]]]
+    groups = [[[a1, b1], [a2[0], b2[0]]]]
     for i in range(max(len(za), len(yb))):
-        g = [a2[o] for o in (za[i] if i < len(za) else [])]
-        groups.append(g + [b2[o] for o in (yb[i] if i < len(yb) else [])])
+        az, by = (za[i] if i < len(za) else []), (yb[i] if i < len(yb) else [])
+        g = [[] for _ in range(max(len(az), len(by)))]
+        for part, offs in ((a2, az), (b2, by)):
+            for k, o in enumerate(offs):
+                g[k].append(part[o])
+        groups.append(g)
     rounds = []
     for gi, g in enumerate(groups):
-        for t in range(max(s.steps for s in g)):
+        for t in range(max(s.steps for e in g for s in e)):
+            events = [[(s, t) for s in e] for e in g]
             if gi > 0 and t == 0 and len(rounds) > 1:
-                rounds[-1] += [(s, t) for s in g]
+                for k, e in enumerate(events):
+                    if k < len(rounds[-1]):
+                        rounds[-1][k] += e
+                    else:
+                        rounds[-1].append(e)
             else:
-                rounds.append([(s, t) for s in g])
+                rounds.append(events)
     last = len(rounds) - 1
     z_round, y_round = min(2, last), min(6, last)
     row_streams = []
@@ -453,14 +462,26 @@
                 if not everything:
                     break
 
-    pending = []
-    globals_done = False
-    for n, todo in enumerate(rounds):
-        for s, t in todo:
+    def start(event):
+        for s, t in event:
             if t == 0 and s.off != 0:
                 (a1 if s.axis == "y" else b1).need(s.off)
             for d in (1, -1):
                 s.send(d, t)
+
+    def arrivals(event):
+        out = []
+        for s, t in event:
+            out += s.arrivals(t)
+        return out
+
+    globals_done = False
+    for n, events in enumerate(rounds):
+        before = rounds[n - 1] if n > 0 else []
+        together = n <= min(1, last)
+        if together:
+            for event in events:
+                start(event)
         if n == 0:
             send_candidates()
         if n == z_round:
@@ -470,23 +491,23 @@
             push_rows(True)
             pick_y()
             row_streams.append([r2, 0])
-        push_rows()
         if n == min(1, last):
             wait_q()
             attend_own()
-        if n > 0:
-            arrived = []
-            for s, t in pending:
-                arrived += s.arrivals(t)
-            if n == y_round + 5:
+        for k in range(max(len(events), len(before))):
+            if not together and k < len(events):
+                start(events[k])
+            if k == 0:
+                push_rows()
+            arrived = arrivals(before[k]) if k < len(before) else []
+            if n == y_round + 5 and k == 0:
                 push_rows(True)
                 arrived += global_entries()
                 globals_done = True
             absorb(arrived)
-        pending = todo
     arrived = []
-    for s, t in pending:
-        arrived += s.arrivals(t)
+    for event in rounds[-1]:
+        arrived += arrivals(event)
     if not globals_done:
         push_rows(True)
         arrived += global_entries()

time: 180 us -> 176 us (0.978)
  Pallas kernels: 174 us -> 170 us
    pallas_call x1, Pallas kernels: 174 us -> 170 us  [shards(): pl.pallas_call(functools.partial(body, nz, ny, nh), out_shape=jax.ShapeDt...]
where the time goes in v3:
time: 176 us; the launch traced here: 175 us
  Pallas kernels  170 us (97%)
  local copies, waits for them, and re-layouts  3.39 us (2%)
    pallas_call x1, Pallas kernels, shards(): pl.pallas_call(functools.partial(body, nz, ny, nh), out_shape=jax.ShapeDt...  170 us

profile of v3, /device:TPU:1, one launch (start us, length us, event | category | flops | bytes accessed | tf_op | source)
XLA Modules:
  0.0 175.2 jit_solution(7265923052247698489)
XLA Ops:
  0.0 0.7 slice_bitcast_fusion
  0.7 0.8 copy.10
  1.5 0.2 and_select_fusion.1
  1.7 0.7 select_reduce_fusion
  2.4 0.7 fusion.2.codes_ref
  3.1 170.1 %page_attention.1 = bf16[96,3072]{1,0:T(8,128)(2,1)} custom-call(s32[64,64]{1,0:T(8,128)} %fusion.2.codes_ref, s32[2]{0:T(128)} %gblk_ref.1, bf16[96,3072]{1,0:T(8,128)(2,1)} %q_ref.1, bf16[96,3072]{1,0:T(8,128)(2,1)} %k_ref.1, bf16[96,3072]{1,0:T(8,128)(2,1)} %v_ref.1), custom_call_target="tpu_custom_call" | custom-call | tf_op jit(solution)/shard_map/page_attention/pallas_call | solution.py:549
  173.3 1.9 %copy.12 = bf16[96,3072]{1,0:T(8,128)(2,1)} copy(bf16[96,3072]{1,0:T(8,128)(2,1)} %page_attention.1) | data formatting | bytes 1179648
  (1 shorter events, 0.0 us)

commit v4 on v3

--- a/solution.py
+++ b/solution.py
@@ -128,9 +128,6 @@
     wait_k = spread("k", k_ref, kx)
     wait_v = spread("v", v_ref, vx)
     wait_q = spread("q", q_ref, qx)
-    wait_k()
-    wait_v()
-
     start1 = codes_ref[me, me]
 
     def choose(index, options):
@@ -139,7 +136,8 @@
             out = jnp.where(index == value, load(), out)
         return out
 
-    for kv, src in enumerate((kx, vx)):
+    for kv, (src, wait) in enumerate(((kx, wait_k), (vx, wait_v))):
+        wait()
         for part, g in enumerate((ga, gb)):
             lo = part * half
             g[me, 0, kv] = src[lo : lo + half, :]
@@ -303,7 +301,7 @@
         for h in range(n_heads):
             for lo in range(b * tile, (b + 1) * tile, BLK):
                 at = slice(lo, lo + BLK)
-                out = mixed[h, :, at] / totals[h, :, at]
+                out = mixed[h, :, at] * (1.0 / totals[h, :, at])
                 ob[at, h * HD : (h + 1) * HD] = out.T.astype(jnp.bfloat16)
         for p in range(b * tile // rl, (b + 1) * tile // rl):
 

time: 176 us -> 176 us (level)
  no operation moved by 1% of the time
where the time goes in v4:
time: 176 us; the launch traced here: 175 us
  Pallas kernels  170 us (97%)
  local copies, waits for them, and re-layouts  3.39 us (2%)
    pallas_call x1, Pallas kernels, shards(): pl.pallas_call(functools.partial(body, nz, ny, nh), out_shape=jax.ShapeDt...  170 us

profile of v4, /device:TPU:1, one launch (start us, length us, event | category | flops | bytes accessed | tf_op | source)
XLA Modules:
  0.0 175.1 jit_solution(15021864675224217309)
XLA Ops:
  0.0 0.7 slice_bitcast_fusion
  0.7 0.8 copy.10
  1.5 0.2 and_select_fusion.1
  1.7 0.7 select_reduce_fusion
  2.4 0.7 fusion.2.codes_ref
  3.1 170.1 %page_attention.1 = bf16[96,3072]{1,0:T(8,128)(2,1)} custom-call(s32[64,64]{1,0:T(8,128)} %fusion.2.codes_ref, s32[2]{0:T(128)} %gblk_ref.1, bf16[96,3072]{1,0:T(8,128)(2,1)} %q_ref.1, bf16[96,3072]{1,0:T(8,128)(2,1)} %k_ref.1, bf16[96,3072]{1,0:T(8,128)(2,1)} %v_ref.1), custom_call_target="tpu_custom_call" | custom-call | tf_op jit(solution)/shard_map/page_attention/pallas_call | solution.py:547
  173.2 1.9 %copy.12 = bf16[96,3072]{1,0:T(8,128)(2,1)} copy(bf16[96,3072]{1,0:T(8,128)(2,1)} %page_attention.1) | data formatting | bytes 1179648
  (1 shorter events, 0.0 us)
